TPU v7x, 512 devices: a whole 4x8x8 slice. The times are simulated.
512 devices in a mesh: frame: 16 (over y, core), tok: 32 (over x, z).
Axes of the slice: x: 4, y: 8, z: 8, core: 2. Of those that a mesh axis runs over, the one named last changes fastest.
Arguments:
- inputs: bfloat16 [16, 24576, 512], P('frame', 'tok'), may hold values from -16 to 16
- kv_weight: bfloat16 [512, 2048], replicated, may hold values from -0.25 to 0.25
- latent_queries: bfloat16 [1024, 1024], P('tok'), may hold values from -21 to 21
- mix_gain: float32 [3072], replicated, may hold values from 0.5 to 2
- mix_weight: bfloat16 [3072, 1024], P(None, 'tok'), may hold values from -0.109375 to 0.109375
- output_queries: bfloat16 [16, 4096, 1024], P('frame', 'tok'), may hold values from -28 to 28
Outputs:
- decoded: float32 [16, 4096, 1024], P('frame', 'tok')
All inputs are finite; a program needn't handle non-finite values.
Results may differ from a plain program's by a relative error of at most 0.035.
Values may be sent and summed in bfloat16 or wider, within the bound.
No kernel may reach another device: no remote copies, remote signals or barrier semaphores. Data moves between devices by JAX's collectives and lax.ppermute only.
A program may use at most 128 MiB of HBM per device.

v0:
```python
import math
import jax
import jax.numpy as jnp
from jax import lax
from jax.sharding import PartitionSpec as P

HEADS = 8
HEAD_DIM = 128


def from_behind(block, axis, distance):
    devices = range(lax.axis_size(axis))
    route = [(i - distance, i) for i in devices if i - distance in devices]
    return lax.ppermute(block, axis, route)


def attend_heads(queries, keys, values, head_count, head_dim):
    maxima = []
    numers = []
    denoms = []
    for head_index in range(head_count):
        low_col = head_index * head_dim
        high_col = low_col + head_dim
        scores = lax.dot_general(
            queries[:, low_col:high_col],
            keys[:, low_col:high_col],
            (((1,), (1,)), ((), ())),
            preferred_element_type=jnp.float32,
        ) / math.sqrt(head_dim)
        row_peak = jnp.max(scores, axis=1)
        weights = jnp.exp(scores - row_peak[:, None])
        denoms.append(jnp.sum(weights, axis=1))
        numers.append(
            jnp.dot(
                weights.astype(jnp.bfloat16),
                values[:, low_col:high_col],
                preferred_element_type=jnp.float32,
            )
        )
        maxima.append(row_peak)
    return (jnp.stack(maxima, axis=1), jnp.concatenate(numers, axis=1), jnp.stack(denoms, axis=1))


def finish_latents(numerator, denominator, head_count, head_dim):
    row_count = numerator.shape[0]
    shaped = numerator.reshape(row_count, head_count, head_dim) / denominator[:, :, None]
    return shaped.reshape(row_count, head_count * head_dim).astype(jnp.bfloat16)


def project_cols(latent_part, gain_part, weight_part):
    scaled = (latent_part.astype(jnp.float32) * gain_part).astype(jnp.bfloat16)
    return lax.dot_general(
        weight_part, scaled, (((0,), (1,)), ((), ())), preferred_element_type=jnp.float32
    )


def local(inputs, kv_weight, latent_queries, mix_gain, mix_weight, output_queries):
    head_count = HEADS
    head_dim = HEAD_DIM
    latent_width = head_count * head_dim
    frame_inputs = inputs[0]
    queries = lax.all_gather(latent_queries, "tok", axis=0, tiled=True)
    key_values = jnp.dot(frame_inputs, kv_weight, preferred_element_type=jnp.float32).astype(
        jnp.bfloat16
    )
    maxima, numers, denoms = attend_heads(
        queries, key_values[:, :latent_width], key_values[:, latent_width:], head_count, head_dim
    )
    peak_all = lax.pmax(maxima.astype(jnp.bfloat16), "tok").astype(maxima.dtype)
    rescale = jnp.exp(maxima - peak_all)
    latent_count = queries.shape[0]
    numer_terms = (
        numers.reshape(latent_count, head_count, head_dim) * rescale[:, :, None]
    ).reshape(latent_count, latent_width)
    denom_terms = denoms * rescale
    numerator, denominator = (
        lax.psum(numer_terms.astype(jnp.bfloat16), "tok").astype(jnp.float32),
        lax.psum(denom_terms.astype(jnp.bfloat16), "tok").astype(jnp.float32),
    )
    latents = finish_latents(numerator, denominator, head_count, head_dim)
    prior_one = from_behind(latents, "frame", 1)
    prior_two = from_behind(latents, "frame", 2)
    joined = jnp.concatenate([latents, prior_one, prior_two], axis=1)
    joined_f32 = joined.astype(jnp.float32)
    squares = jnp.sum(joined_f32 * joined_f32, axis=1)
    summed = project_cols(joined, mix_gain, mix_weight)
    inverse = lax.rsqrt(squares / (3 * latent_width) + 1e-06)
    mixed_cols = jax.nn.gelu(summed * inverse[None, :], approximate=False).astype(jnp.bfloat16)
    mixed_t = lax.all_gather(mixed_cols, "tok", axis=0, tiled=True)
    frame_queries = output_queries[0]
    pieces = []
    for head_index in range(head_count):
        low_col = head_index * head_dim
        high_col = low_col + head_dim
        scores = jnp.dot(
            frame_queries[:, low_col:high_col],
            mixed_t[low_col:high_col],
            preferred_element_type=jnp.float32,
        ) / math.sqrt(head_dim)
        row_peak = jnp.max(scores, axis=1)
        weights = jnp.exp(scores - row_peak[:, None])
        denom_sum = jnp.sum(weights, axis=1)
        head_sum = lax.dot_general(
            weights.astype(jnp.bfloat16),
            mixed_t[low_col:high_col],
            (((1,), (1,)), ((), ())),
            preferred_element_type=jnp.float32,
        )
        pieces.append(head_sum / denom_sum[:, None])
    result = jnp.concatenate(pieces, axis=1)
    return result[None]


def solution(mesh):
    return jax.shard_map(
        local,
        mesh=mesh,
        in_specs=(
            P("frame", "tok", None),
            P(),
            P("tok", None),
            P(),
            P(None, "tok"),
            P("frame", "tok", None),
        ),
        out_specs=P("frame", "tok", None),
        check_vma=False,
    )
```

profile of v0, /device:TPU:8, one launch (start us, length us, event | category | flops | bytes accessed | tf_op | source)
XLA Modules:
  0.0 638.2 jit_solution(1912989845370051976)
XLA Ops:
  8.1 4.6 convolution_convert_fusion
  12.7 86.4 %all-gather.3.cloned.1.call-done = bf16[1024,1024]{1,0:T(8,128)(2,1)} async-done(((bf16[32,1024]{1,0:T(8,128)(2,1)}), bf16[1024,1024]{1,0:T(8,128)(2,1)}) %all-gather.3.cloned.1.call-update) | async-done | bytes 2097168 | tf_op jit(solution)/shard_map/all_gather | solution.py:62
  101.3 2.4 fusion.55
  105.9 2.1 multiply_reduce_fusion.5
  114.0 2.1 multiply_reduce_fusion.2
  116.6 2.1 multiply_reduce_fusion.1
  123.8 140.2 %pmax.7 = bf16[1024,8]{0,1:T(8,128)(2,1)S(1)} all-reduce(bf16[1024,8]{0,1:T(8,128)(2,1)S(1)} %convert_element_type.107), channel_id=1, replica_groups=mesh['frame'=16,'tok'=32] {'tok'}, use_global_device_ids=true, to_apply=%region_8.0 | all-reduce | flops 8192 | bytes 32768 | tf_op jit(solution)/shard_map/pmax | solution.py:69
  264.0 3.6 fusion.58
  267.6 2.6 fusion.61
  270.2 2.6 fusion.64
  272.8 2.6 fusion.67
  275.4 2.6 fusion.70
  278.0 2.4 fusion.73
  280.4 2.4 fusion.76
  282.9 4.1 fusion.6
  287.1 138.0 %psum.15 = bf16[1024,8]{0,1:T(8,128)(2,1)S(1)} all-reduce(bf16[1024,8]{0,1:T(8,128)(2,1)S(1)} %get-tuple-element.5), channel_id=1, replica_groups=mesh['frame'=16,'tok'=32] {'tok'}, use_global_device_ids=true, to_apply=%region_18.0 | all-reduce | flops 8192 | bytes 32768 | tf_op jit(solution)/shard_map/psum | solution.py:78
  425.1 21.8 %all-reduce.2.cloned.1.call-done = bf16[1024,1024]{0,1:T(8,128)(2,1)} async-done(((bf16[1024,1024]{0,1:T(8,128)(2,1)}), bf16[1024,1024]{0,1:T(8,128)(2,1)}) %all-reduce.2.cloned.1.call-update) | async-done | bytes 2097168 | tf_op jit(solution)/shard_map/psum | solution.py:77
  446.9 2.2 fusion.5
  451.2 3.6 collective-permute-start.1
  454.8 41.8 %collective-permute-done = bf16[1024,1024]{0,1:T(8,128)(2,1)S(1)} collective-permute-done((bf16[1024,1024]{0,1:T(8,128)(2,1)S(1)}, bf16[1024,1024]{0,1:T(8,128)(2,1)S(1)}, u32[]{:S(2)}, u32[]{:S(2)}) %collective-permute-start) | collective-permute-done | bytes 2097184 | tf_op jit(solution)/shard_map/ppermute | solution.py:14
  496.6 5.0 collective-permute-done.1
  501.6 11.4 %fusion.1 = f32[1024]{0:T(1024)S(1)} fusion(bf16[1024,1024]{0,1:T(8,128)(2,1)S(1)} %collective-permute-done.1, bf16[1024,1024]{0,1:T(8,128)(2,1)S(1)} %collective-permute-done, bf16[1024,1024]{0,1:T(8,128)(2,1)S(1)} %fusion.5), kind=kLoop, calls=%fused_computation.3 | loop fusion | flops 25164800 | bytes 6295552 | tf_op jit(solution)/shard_map/reduce_sum | solution.py:85
  513.0 2.4 fusion.173
  515.4 101.5 %all-gather.5.cloned.1.call-done = bf16[1024,1024]{1,0:T(8,128)(2,1)} async-done(((bf16[32,1024]{1,0:T(8,128)(2,1)}), bf16[1024,1024]{1,0:T(8,128)(2,1)}) %all-gather.5.cloned.1.call-update) | async-done | bytes 2097168 | tf_op jit(solution)/shard_map/all_gather | solution.py:89
  (85 shorter events, 34.3 us)
Async XLA Ops:
  6.5 1.6 copy-start
  6.5 92.6 %all-gather.3.cloned.1.call-start = ((), (), s32[]{:S(2)}) async-start(), calls=%async_computation | async-start | bytes 2162688 | tf_op jit(solution)/shard_map/all_gather | solution.py:62
  7.3 439.6 %all-reduce.2.cloned.1.call-start = ((), (), s32[]{:S(2)}) async-start(), calls=%async_computation.1 | async-start | bytes 4194304 | tf_op jit(solution)/shard_map/psum | solution.py:77
  105.4 2.7 copy-start.1
  108.1 2.7 copy-start.2
  110.7 2.7 copy-start.4
  113.4 2.7 copy-start.6
  116.1 2.7 copy-start.8
  118.8 2.7 copy-start.10
  121.4 1.7 copy-start.12
  264.0 3.6 copy-start.3
  264.0 6.2 copy-start.5
  267.6 5.2 copy-start.7
  270.2 5.2 copy-start.9
  272.8 5.2 copy-start.11
  275.4 5.0 copy-start.13
  287.1 329.9 %all-gather.5.cloned.1.call-start = ((), (), s32[]{:S(2)}) async-start(), calls=%async_computation.2 | async-start | bytes 2162688 | tf_op jit(solution)/shard_map/all_gather | solution.py:89
  449.1 63.9 %copy-start.15 = (bf16[3072,32]{0,1:T(8,128)(2,1)S(1)}, bf16[3072,32]{0,1:T(8,128)(2,1)}, u32[]{:S(2)}) copy-start(bf16[3072,32]{0,1:T(8,128)(2,1)} %param.10) | copy-start | bytes 589828
  449.1 63.9 %copy-start.16 = (f32[3072]{0:T(1024)S(1)}, f32[3072]{0:T(1024)}, u32[]{:S(2)}) copy-start(f32[3072]{0:T(1024)} %param.9) | copy-start | bytes 36868
  449.1 47.4 %collective-permute-start = (bf16[1024,1024]{0,1:T(8,128)(2,1)S(1)}, bf16[1024,1024]{0,1:T(8,128)(2,1)S(1)}, u32[]{:S(2)}, u32[]{:S(2)}) collective-permute-start(bf16[1024,1024]{0,1:T(8,128)(2,1)S(1)} %fusion.5), channel_id=1, source_target_pairs={{0,32},{32,64},{64,96},{96,128},{128,160},{160,192},{192,224},{224... | collective-permute-start | bytes 6291464 | tf_op jit(solution)/shard_map/ppermute | solution.py:14
  451.2 50.4 %collective-permute-start.1 = (bf16[1024,1024]{0,1:T(8,128)(2,1)S(1)}, bf16[1024,1024]{0,1:T(8,128)(2,1)S(1)}, u32[]{:S(2)}, u32[]{:S(2)}) collective-permute-start(bf16[1024,1024]{0,1:T(8,128)(2,1)S(1)} %fusion.5), channel_id=1, source_target_pairs={{0,64},{32,96},{64,128},{96,160},{128,192},{160,224},{192,256},{22... | collective-permute-start | bytes 6291464 | tf_op jit(solution)/shard_map/ppermute | solution.py:14
  622.5 6.1 copy-start.14
Sparse Core Ops, SparseCore 0:
  10.5 88.5 all-gather.2
  287.2 159.6 all-reduce.1
  515.5 101.3 all-gather.4
where the time goes:
time: 639 us; the launch traced here: 638 us
  blocking collectives  278 us (44%)
  waiting for transfers between devices  257 us (40%)
  matrix products  56.4 us (9%)
  other arithmetic  23.4 us (4%)
  between operations  13.4 us (2%)
    pmax x1, blocking collectives, local(): peak_all = lax.pmax(maxima.astype(jnp.bfloat16), 'tok').astype(maxima.dtype)  140 us
    psum x1, blocking collectives, local(): lax.psum(denom_terms.astype(jnp.bfloat16), 'tok').astype(jnp.float32)  138 us
    all_gather x1, waiting for transfers between devices, local(): mixed_t = lax.all_gather(mixed_cols, 'tok', axis=0, tiled=True)  102 us
    all_gather x1, waiting for transfers between devices, local(): queries = lax.all_gather(latent_queries, 'tok', axis=0, tiled=True)  86.4 us
    ppermute x2, waiting for transfers between devices, from_behind(): return lax.ppermute(block, axis, route)  46.8 us
    psum x1, waiting for transfers between devices, local(): lax.psum(numer_terms.astype(jnp.bfloat16), 'tok').astype(jnp.float32)  21.8 us
    dot_general x8, matrix products, attend_heads(): jnp.dot(weights.astype(jnp.bfloat16), values[:, low_col:high_col], prefer...  21.2 us
    dot_general x8, matrix products, attend_heads(): lax.dot_general(queries[:, low_col:high_col], keys[:, low_col:high_col],...  15.8 us
  transfers between devices with their start and end apart: 5, of which 5 were waited for; matrix products, arithmetic and copies ran while one was open for 1% of the time, Pallas kernels for 0%

commit v1 on v0

--- a/solution.py
+++ b/solution.py
@@ -86,7 +86,10 @@
     summed = project_cols(joined, mix_gain, mix_weight)
     inverse = lax.rsqrt(squares / (3 * latent_width) + 1e-06)
     mixed_cols = jax.nn.gelu(summed * inverse[None, :], approximate=False).astype(jnp.bfloat16)
-    mixed_t = lax.all_gather(mixed_cols, "tok", axis=0, tiled=True)
+    peers = lax.axis_size("tok")
+    blocks = jnp.stack([mixed_cols for _ in range(peers)])
+    blocks = lax.all_to_all(blocks, "tok", split_axis=0, concat_axis=0)
+    mixed_t = jnp.concatenate(blocks, axis=0)
     frame_queries = output_queries[0]
     pieces = []
     for head_index in range(head_count):

time: 639 us -> 589 us (0.922)
  the two profiles are of different devices: /device:TPU:8 before, /device:TPU:97 now
where the time goes in v1:
time: 589 us; the launch traced here: 588 us
  blocking collectives  261 us (44%)
  waiting for transfers between devices  227 us (39%)
  matrix products  48 us (8%)
  other arithmetic  23.4 us (4%)
  between operations  13.8 us (2%)
  starting transfers between devices  9.94 us (2%)
    psum x1, blocking collectives, local(): lax.psum(denom_terms.astype(jnp.bfloat16), 'tok').astype(jnp.float32)  113 us
    pmax x1, blocking collectives, local(): peak_all = lax.pmax(maxima.astype(jnp.bfloat16), 'tok').astype(maxima.dtype)  109 us
    all_gather x1, waiting for transfers between devices, local(): queries = lax.all_gather(latent_queries, 'tok', axis=0, tiled=True)  79.8 us
    psum x1, waiting for transfers between devices, local(): lax.psum(numer_terms.astype(jnp.bfloat16), 'tok').astype(jnp.float32)  78 us
    ppermute x2, waiting for transfers between devices, from_behind(): return lax.ppermute(block, axis, route)  68.3 us
    all_to_all x1, blocking collectives, local(): blocks = lax.all_to_all(blocks, 'tok', split_axis=0, concat_axis=0)  38.8 us
    dot_general x8, matrix products, attend_heads(): jnp.dot(weights.astype(jnp.bfloat16), values[:, low_col:high_col], prefer...  21.2 us
    dot_general x8, matrix products, attend_heads(): lax.dot_general(queries[:, low_col:high_col], keys[:, low_col:high_col],...  15.8 us
  transfers between devices with their start and end apart: 4, of which 4 were waited for; matrix products, arithmetic and copies ran while one was open for 1% of the time, Pallas kernels for 0%

profile of v1, /device:TPU:97, one launch (start us, length us, event | category | flops | bytes accessed | tf_op | source)
XLA Modules:
  0.0 587.8 jit_solution(7069232143020674691)
XLA Ops:
  8.1 4.6 convolution_convert_fusion
  12.7 79.8 %all-gather.2.cloned.1.call-done = bf16[1024,1024]{1,0:T(8,128)(2,1)} async-done(((bf16[32,1024]{1,0:T(8,128)(2,1)}), bf16[1024,1024]{1,0:T(8,128)(2,1)}) %all-gather.2.cloned.1.call-update) | async-done | bytes 2097168 | tf_op jit(solution)/shard_map/all_gather | solution.py:62
  94.8 2.4 fusion.55
  99.4 2.1 multiply_reduce_fusion.5
  102.1 2.1 multiply_reduce_fusion.4
  107.4 2.1 multiply_reduce_fusion.2
  117.2 109.3 %pmax.7 = bf16[1024,8]{0,1:T(8,128)(2,1)S(1)} all-reduce(bf16[1024,8]{0,1:T(8,128)(2,1)S(1)} %convert_element_type.107), channel_id=1, replica_groups=mesh['frame'=16,'tok'=32] {'tok'}, use_global_device_ids=true, to_apply=%region_8.0 | all-reduce | flops 8192 | bytes 32768 | tf_op jit(solution)/shard_map/pmax | solution.py:69
  226.5 3.6 fusion.58
  230.1 2.6 fusion.61
  232.7 2.6 fusion.64
  235.3 2.6 fusion.67
  237.8 2.6 fusion.70
  240.4 2.4 fusion.73
  242.9 2.4 fusion.76
  245.4 4.1 fusion.6
  249.5 112.8 %psum.15 = bf16[1024,8]{0,1:T(8,128)(2,1)S(1)} all-reduce(bf16[1024,8]{0,1:T(8,128)(2,1)S(1)} %get-tuple-element.5), channel_id=1, replica_groups=mesh['frame'=16,'tok'=32] {'tok'}, use_global_device_ids=true, to_apply=%region_18.0 | all-reduce | flops 8192 | bytes 32768 | tf_op jit(solution)/shard_map/psum | solution.py:78
  362.3 78.0 %all-reduce.2.cloned.1.call-done = bf16[1024,1024]{0,1:T(8,128)(2,1)} async-done(((bf16[1024,1024]{0,1:T(8,128)(2,1)}), bf16[1024,1024]{0,1:T(8,128)(2,1)}) %all-reduce.2.cloned.1.call-update) | async-done | bytes 2097168 | tf_op jit(solution)/shard_map/psum | solution.py:77
  440.3 2.2 fusion.5
  442.6 7.5 %collective-permute-start = (bf16[1024,1024]{0,1:T(8,128)(2,1)S(1)}, bf16[1024,1024]{0,1:T(8,128)(2,1)S(1)}, u32[]{:S(2)}, u32[]{:S(2)}) collective-permute-start(bf16[1024,1024]{0,1:T(8,128)(2,1)S(1)} %fusion.5), channel_id=1, source_target_pairs={{0,32},{32,64},{64,96},{96,128},{128,160},{160,192},{192,224},{224... | collective-permute-start | bytes 6291464 | tf_op jit(solution)/shard_map/ppermute | solution.py:14
  450.0 2.4 collective-permute-start.1
  452.5 40.5 %collective-permute-done = bf16[1024,1024]{0,1:T(8,128)(2,1)S(1)} collective-permute-done((bf16[1024,1024]{0,1:T(8,128)(2,1)S(1)}, bf16[1024,1024]{0,1:T(8,128)(2,1)S(1)}, u32[]{:S(2)}, u32[]{:S(2)}) %collective-permute-start) | collective-permute-done | bytes 2097184 | tf_op jit(solution)/shard_map/ppermute | solution.py:14
  492.9 27.8 %collective-permute-done.1 = bf16[1024,1024]{0,1:T(8,128)(2,1)S(1)} collective-permute-done((bf16[1024,1024]{0,1:T(8,128)(2,1)S(1)}, bf16[1024,1024]{0,1:T(8,128)(2,1)S(1)}, u32[]{:S(2)}, u32[]{:S(2)}) %collective-permute-start.1) | collective-permute-done | bytes 2097184 | tf_op jit(solution)/shard_map/ppermute | solution.py:14
  520.7 11.4 %fusion.1 = f32[1024]{0:T(1024)S(1)} fusion(bf16[1024,1024]{0,1:T(8,128)(2,1)S(1)} %collective-permute-done.1, bf16[1024,1024]{0,1:T(8,128)(2,1)S(1)} %collective-permute-done, bf16[1024,1024]{0,1:T(8,128)(2,1)S(1)} %fusion.5), kind=kLoop, calls=%fused_computation.3 | loop fusion | flops 25164800 | bytes 6295552 | tf_op jit(solution)/shard_map/reduce_sum | solution.py:85
  534.2 38.8 %all_to_all.5 = bf16[32,32,1024]{2,1,0:T(8,128)(2,1)S(1)} all-to-all(bf16[32,32,1024]{2,1,0:T(8,128)(2,1)S(1)} %stack.32), channel_id=1, replica_groups=mesh['frame'=16,'tok'=32] {'tok'}, dimensions={0} | all-to-all | bytes 4194304 | tf_op jit(solution)/shard_map/all_to_all | solution.py:91
  (85 shorter events, 27.4 us)
Async XLA Ops:
  6.5 1.6 copy-start
  6.5 86.0 %all-gather.2.cloned.1.call-start = ((), (), s32[]{:S(2)}) async-start(), calls=%async_computation.1 | async-start | bytes 2162688 | tf_op jit(solution)/shard_map/all_gather | solution.py:62
  7.3 433.1 %all-reduce.2.cloned.1.call-start = ((), (), s32[]{:S(2)}) async-start(), calls=%async_computation.2 | async-start | bytes 4194304 | tf_op jit(solution)/shard_map/psum | solution.py:77
  98.8 2.7 copy-start.1
  101.5 2.7 copy-start.2
  104.2 2.7 copy-start.4
  106.9 2.7 copy-start.6
  109.5 2.7 copy-start.8
  112.2 2.7 copy-start.10
  114.9 1.7 copy-start.12
  226.5 3.6 copy-start.3
  226.5 6.2 %copy-start.5 = (f32[768,1024]{1,0:T(8,128)S(1)}, f32[768,1024]{1,0:T(8,128)}, u32[]{:S(2)}) copy-start(f32[768,1024]{1,0:T(8,128)} %copy-done.4) | copy-start | bytes 9437188
  230.1 5.2 copy-start.7
  232.7 5.2 copy-start.9
  235.3 5.2 copy-start.11
  237.8 5.0 copy-start.13
  442.5 89.6 %copy-start.15 = (bf16[3072,32]{0,1:T(8,128)(2,1)S(1)}, bf16[3072,32]{0,1:T(8,128)(2,1)}, u32[]{:S(2)}) copy-start(bf16[3072,32]{0,1:T(8,128)(2,1)} %param.10) | copy-start | bytes 589828
  442.5 89.6 %copy-start.16 = (f32[3072]{0:T(1024)S(1)}, f32[3072]{0:T(1024)}, u32[]{:S(2)}) copy-start(f32[3072]{0:T(1024)} %param.9) | copy-start | bytes 36868
  442.6 50.4 %collective-permute-start = (bf16[1024,1024]{0,1:T(8,128)(2,1)S(1)}, bf16[1024,1024]{0,1:T(8,128)(2,1)S(1)}, u32[]{:S(2)}, u32[]{:S(2)}) collective-permute-start(bf16[1024,1024]{0,1:T(8,128)(2,1)S(1)} %fusion.5), channel_id=1, source_target_pairs={{0,32},{32,64},{64,96},{96,128},{128,160},{160,192},{192,224},{224... | collective-permute-start | bytes 6291464 | tf_op jit(solution)/shard_map/ppermute | solution.py:14
  450.0 70.7 %collective-permute-start.1 = (bf16[1024,1024]{0,1:T(8,128)(2,1)S(1)}, bf16[1024,1024]{0,1:T(8,128)(2,1)S(1)}, u32[]{:S(2)}, u32[]{:S(2)}) collective-permute-start(bf16[1024,1024]{0,1:T(8,128)(2,1)S(1)} %fusion.5), channel_id=1, source_target_pairs={{0,64},{32,96},{64,128},{96,160},{128,192},{160,224},{192,256},{22... | collective-permute-start | bytes 6291464 | tf_op jit(solution)/shard_map/ppermute | solution.py:14
  573.0 1.0 copy-start.14
Sparse Core Ops, SparseCore 0:
  10.5 82.0 all-gather.1
  249.6 190.6 all-reduce.1
